TPU v7x, 32 devices: a whole 2x2x4 slice. The times are simulated.
32 devices in a mesh: dp: 8 (over y, x, core), replica: 4 (over z).
Axes of the slice: x: 2, y: 2, z: 4, core: 2. Of those that a mesh axis runs over, the one named last changes fastest.
Arguments:
- gradient: bfloat16 [4, 8, 8, 8192], P('replica', 'dp'), may hold values from -6 to 6
- master: float32 [8, 8192], P('dp', 'replica'), may hold values from -0.0625 to 0.0625
- moment: float32 [8, 8192], P('dp', 'replica'), may hold values from -0.046875 to 0.046875
- second: float32 [8, 8192], P('dp', 'replica'), may hold values from 1e-06 to 0.0001
Outputs:
- new_params: bfloat16 [8, 8192], P('dp')
- new_master: float32 [8, 8192], P('dp', 'replica')
- new_moment: float32 [8, 8192], P('dp', 'replica')
- new_second: float32 [8, 8192], P('dp', 'replica')
- direction: float32 [8, 8192], P('dp', 'replica')
- ratios: float32 [4], replicated
All inputs are finite; a program needn't handle non-finite values.
Results may differ from a plain program's by a relative error of at most 0.001.
Values may be sent and summed in bfloat16 or wider, within the bound.
A program may use at most 64 MiB of HBM per device.

v0:
```python
import jax
import jax.numpy as jnp
from jax import lax
from jax.sharding import PartitionSpec as P

MATS = 4
STEP = 2


def local(gradient, master, moment, second):
    raw_rows = gradient[0, 0]
    rows_all, width = raw_rows.shape
    data_count = lax.axis_size("dp")
    rep_count = lax.axis_size("replica")
    row_dev = rows_all // data_count
    terms = raw_rows.astype(jnp.float32)
    owned_rows = lax.psum_scatter(terms, "dp", scatter_dimension=0, tiled=True)
    summed = lax.psum_scatter(owned_rows, "replica", scatter_dimension=1, tiled=True)
    grad = summed / (data_count * rep_count)
    new_moment = 0.9 * moment + 0.1 * grad
    new_second = 0.999 * second + 0.001 * grad * grad
    first_fix = 1.0 - 0.9**STEP
    second_fix = 1.0 - 0.999**STEP
    direction = new_moment / first_fix / (jnp.sqrt(new_second / second_fix) + 1e-08)
    new_master = master - 0.0003 * (direction + 0.1 * master)
    row_ids = lax.axis_index("dp") * row_dev + lax.iota(jnp.int32, row_dev)
    owner_mat = row_ids // (rows_all // MATS)
    member = (owner_mat[:, None] == lax.iota(jnp.int32, MATS)[None, :]).astype(jnp.float32)
    dir_rows = jnp.sum(direction * direction, axis=1)
    wgt_rows = jnp.sum(master * master, axis=1)
    dir_part = jnp.sum(member * dir_rows[:, None], axis=0)
    wgt_part = jnp.sum(member * wgt_rows[:, None], axis=0)
    dir_sq, wgt_sq = lax.psum((dir_part, wgt_part), ("dp", "replica"))
    ratios = jnp.sqrt(dir_sq) / (jnp.sqrt(wgt_sq) + 1e-06)
    new_params = lax.all_gather(new_master.astype(jnp.bfloat16), "replica", axis=1, tiled=True)
    return (new_params, new_master, new_moment, new_second, direction, ratios)


def solution(mesh):
    return jax.shard_map(
        local,
        mesh=mesh,
        in_specs=(
            P("replica", "dp", None, None),
            P("dp", "replica"),
            P("dp", "replica"),
            P("dp", "replica"),
        ),
        out_specs=(
            P("dp", None),
            P("dp", "replica"),
            P("dp", "replica"),
            P("dp", "replica"),
            P("dp", "replica"),
            P(),
        ),
        check_vma=False,
    )
```

profile of v0, /device:TPU:0, one launch (start us, length us, event | category | flops | bytes accessed | tf_op | source)
XLA Modules:
  0.0 214.0 jit_solution(4225715408327386011)
XLA Ops:
  7.2 0.0 all-reduce.4.cloned.1.call-start
  7.2 1.6 bitcast_convert_fusion
  8.8 0.0 all-reduce.4.cloned.1.call-update
  8.9 0.0 reduce-scatter.4.cloned.1.call-start
  8.9 1.2 dynamic-slice
  10.2 57.2 %all-reduce.4.cloned.1.call-done = f32[8,8192]{1,0:T(8,128)} async-done(((f32[8,8192]{1,0:T(8,128)}), f32[8,8192]{1,0:T(8,128)}) %all-reduce.4.cloned.1.call-update) | async-done | bytes 262160
  67.3 1.6 constant_dynamic-slice_fusion
  68.9 0.0 copy-start.1
  69.0 0.0 copy-start.2
  69.0 0.0 copy-start.3
  69.0 2.6 %copy.10 = f32[1,8192]{0,1:T(8,128)} copy(f32[1,8192]{1,0:T(1,128)S(1)} %constant_dynamic-slice_fusion) | data formatting | bytes 65536
  71.6 0.0 reduce-scatter.4.cloned.1.call-update
  71.6 76.3 %reduce-scatter.4.cloned.1.call-done = f32[2048,1]{1,0:T(8,128)} async-done(((f32[8192,1]{1,0:T(8,128)}), f32[2048,1]{1,0:T(8,128)}) %reduce-scatter.4.cloned.1.call-update) | async-done | bytes 8208
  147.9 1.6 copy.11
  149.5 0.0 copy-done.1
  149.5 0.0 copy-done.2
  149.5 1.3 multiply_reduce_fusion.1
  150.7 0.0 copy-start
  150.7 0.0 copy-done.3
  150.7 1.2 fusion
  152.0 13.7 %all_gather.3 = bf16[1,8192]{1,0:T(2,128)(2,1)S(1)} all-gather(bf16[1,2048]{1,0:T(2,128)(2,1)S(1)} %get-tuple-element.12), channel_id=1, replica_groups=mesh['dp'=8,'replica'=4] {'replica'}, dimensions={1}, use_global_device_ids=true | all-gather | bytes 20480 | tf_op jit(solution)/shard_map/all_gather | solution.py:35
  165.6 1.3 compare_select_fusion
  166.9 39.1 %all-reduce.1 = (f32[4]{0:T(128)S(1)}, f32[4]{0:T(128)S(1)}) all-reduce(f32[4]{0:T(128)S(1)} %get-tuple-element.15, f32[4]{0:T(128)S(1)} %get-tuple-element.16), channel_id=1, replica_groups=mesh['dp'=8,'replica'=4] {'dp','replica'}, use_global_device_ids=true, to_apply=%region_5.6 | all-reduce | flops 8 | bytes 64 | tf_op jit(solution)/shard_map/psum | solution.py:33
  206.0 0.5 add_divide_fusion.1
  206.6 0.6 copy.14
  207.2 0.0 copy-done
Async XLA Ops:
  7.2 60.1 %all-reduce.4.cloned.1.call-start = ((), (), s32[]{:S(2)}) async-start(), calls=%async_computation.2 | async-start | bytes 524288
  8.9 139.1 %reduce-scatter.4.cloned.1.call-start = ((), (), s32[]{:S(2)}) async-start(), calls=%async_computation.1 | async-start | bytes 5242880
  68.9 80.5 %copy-start.1 = (f32[1,2048]{1,0:T(1,128)S(1)}, f32[1,2048]{1,0:T(1,128)}, u32[]{:S(2)}) copy-start(f32[1,2048]{1,0:T(1,128)} %param.6) | copy-start | bytes 24580
  69.0 80.5 %copy-start.2 = (f32[1,2048]{1,0:T(1,128)S(1)}, f32[1,2048]{1,0:T(1,128)}, u32[]{:S(2)}) copy-start(f32[1,2048]{1,0:T(1,128)} %param.7) | copy-start | bytes 24580
  69.0 81.8 %copy-start.3 = (f32[1,2048]{1,0:T(1,128)S(1)}, f32[1,2048]{1,0:T(1,128)}, u32[]{:S(2)}) copy-start(f32[1,2048]{1,0:T(1,128)} %param.5) | copy-start | bytes 24580
  150.7 56.4 %copy-start = (f32[1,2048]{1,0:T(1,128)}, f32[1,2048]{1,0:T(1,128)S(1)}, u32[]{:S(2)}) copy-start(f32[1,2048]{1,0:T(1,128)S(1)} %get-tuple-element.27) | copy-start | bytes 24580
Sparse Core Ops, SparseCore 0:
  11.1 56.2 all-reduce.3
  71.7 76.1 reduce-scatter.3
where the time goes:
time: 214 us
  waiting for transfers between devices  133 us (62%)
  blocking collectives  52.8 us (25%)
  between operations  14.1 us (7%)
  local copies, waits for them, and re-layouts  7.67 us (4%)
  other arithmetic  5.92 us (3%)
    unnamed x4, waiting for transfers between devices  133 us
    psum x1, blocking collectives, local(): dir_sq, wgt_sq = lax.psum((dir_part, wgt_part), ('dp', 'replica'))  39.1 us
    all_gather x1, blocking collectives, local(): lax.all_gather(new_master.astype(jnp.bfloat16), 'replica', axis=1, tiled=...  13.7 us
    unnamed x13, local copies, waits for them, and re-layouts  7.67 us
  transfers between devices with their start and end apart: 2, of which 2 were waited for; matrix products, arithmetic and copies ran while one was open for 1% of the time, Pallas kernels for 0%

commit v1 on v0

--- a/solution.py
+++ b/solution.py
@@ -5,6 +5,10 @@
 
 MATS = 4
 STEP = 2
+
+
+def trace_spans(z_in):
+    return lax.psum(lax.psum(z_in, "replica"), axis_name="dp")
 
 
 def local(gradient, master, moment, second):
@@ -30,7 +34,7 @@
     wgt_rows = jnp.sum(master * master, axis=1)
     dir_part = jnp.sum(member * dir_rows[:, None], axis=0)
     wgt_part = jnp.sum(member * wgt_rows[:, None], axis=0)
-    dir_sq, wgt_sq = lax.psum((dir_part, wgt_part), ("dp", "replica"))
+    dir_sq, wgt_sq = trace_spans((dir_part, wgt_part))
     ratios = jnp.sqrt(dir_sq) / (jnp.sqrt(wgt_sq) + 1e-06)
     new_params = lax.all_gather(new_master.astype(jnp.bfloat16), "replica", axis=1, tiled=True)
     return (new_params, new_master, new_moment, new_second, direction, ratios)

time: 214 us -> 197 us (0.921)
  blocking collectives: 52.8 us -> 35.8 us
    psum x1 -> x2, blocking collectives: 39.1 us -> 22.1 us  [trace_spans(): return lax.psum(lax.psum(z_in, 'replica'), axis_name='dp')]
where the time goes in v1:
time: 197 us
  waiting for transfers between devices  133 us (68%)
  blocking collectives  35.8 us (18%)
  between operations  14.1 us (7%)
  local copies, waits for them, and re-layouts  7.67 us (4%)
  other arithmetic  5.92 us (3%)
    unnamed x4, waiting for transfers between devices  133 us
    psum x2, blocking collectives, trace_spans(): return lax.psum(lax.psum(z_in, 'replica'), axis_name='dp')  22.1 us
    all_gather x1, blocking collectives, local(): lax.all_gather(new_master.astype(jnp.bfloat16), 'replica', axis=1, tiled=...  13.7 us
    unnamed x13, local copies, waits for them, and re-layouts  7.67 us
  transfers between devices with their start and end apart: 2, of which 2 were waited for; matrix products, arithmetic and copies ran while one was open for 1% of the time, Pallas kernels for 0%

profile of v1, /device:TPU:0, one launch (start us, length us, event | category | flops | bytes accessed | tf_op | source)
XLA Modules:
  0.0 197.1 jit_solution(16382237676482239432)
XLA Ops:
  7.2 0.0 all-reduce.5.cloned.1.call-start
  7.2 1.6 bitcast_convert_fusion
  8.8 0.0 all-reduce.5.cloned.1.call-update
  8.9 0.0 reduce-scatter.4.cloned.1.call-start
  8.9 1.2 dynamic-slice
  10.2 57.2 %all-reduce.5.cloned.1.call-done = f32[8,8192]{1,0:T(8,128)} async-done(((f32[8,8192]{1,0:T(8,128)}), f32[8,8192]{1,0:T(8,128)}) %all-reduce.5.cloned.1.call-update) | async-done | bytes 262160
  67.3 1.6 constant_dynamic-slice_fusion
  68.9 0.0 copy-start.1
  69.0 0.0 copy-start.2
  69.0 0.0 copy-start.3
  69.0 2.6 %copy.10 = f32[1,8192]{0,1:T(8,128)} copy(f32[1,8192]{1,0:T(1,128)S(1)} %constant_dynamic-slice_fusion) | data formatting | bytes 65536
  71.6 0.0 reduce-scatter.4.cloned.1.call-update
  71.6 76.3 %reduce-scatter.4.cloned.1.call-done = f32[2048,1]{1,0:T(8,128)} async-done(((f32[8192,1]{1,0:T(8,128)}), f32[2048,1]{1,0:T(8,128)}) %reduce-scatter.4.cloned.1.call-update) | async-done | bytes 8208
  147.9 1.6 copy.11
  149.5 0.0 copy-done.1
  149.5 0.0 copy-done.2
  149.5 1.3 multiply_reduce_fusion.1
  150.7 0.0 copy-start
  150.7 0.0 copy-done.3
  150.7 1.2 fusion
  152.0 13.7 %all_gather.3 = bf16[1,8192]{1,0:T(2,128)(2,1)S(1)} all-gather(bf16[1,2048]{1,0:T(2,128)(2,1)S(1)} %get-tuple-element.14), channel_id=1, replica_groups=mesh['dp'=8,'replica'=4] {'replica'}, dimensions={1}, use_global_device_ids=true | all-gather | bytes 20480 | tf_op jit(solution)/shard_map/all_gather | solution.py:39
  165.6 1.3 compare_select_fusion
  166.9 10.4 %all-reduce.2 = (f32[4]{0:T(128)S(1)}, f32[4]{0:T(128)S(1)}) all-reduce(f32[4]{0:T(128)S(1)} %get-tuple-element.17, f32[4]{0:T(128)S(1)} %get-tuple-element.18), channel_id=1, replica_groups=mesh['dp'=8,'replica'=4] {'replica'}, use_global_device_ids=true, to_apply=%region_6.7 | all-reduce | flops 8 | bytes 64 | tf_op jit(solution)/shard_map/psum | solution.py:11
  177.3 11.8 %all-reduce.1 = (f32[4]{0:T(128)S(1)}, f32[4]{0:T(128)S(1)}) all-reduce(f32[4]{0:T(128)S(1)} %get-tuple-element.8, f32[4]{0:T(128)S(1)} %get-tuple-element.9), channel_id=1, replica_groups=mesh['dp'=8,'replica'=4] {'dp'}, use_global_device_ids=true, to_apply=%region_7.8 | all-reduce | flops 8 | bytes 64 | tf_op jit(solution)/shard_map/psum | solution.py:11
  189.1 0.5 add_divide_fusion.1
  189.6 0.6 copy.14
  190.2 0.0 copy-done
Async XLA Ops:
  7.2 60.1 %all-reduce.5.cloned.1.call-start = ((), (), s32[]{:S(2)}) async-start(), calls=%async_computation.2 | async-start | bytes 524288
  8.9 139.1 %reduce-scatter.4.cloned.1.call-start = ((), (), s32[]{:S(2)}) async-start(), calls=%async_computation.1 | async-start | bytes 5242880
  68.9 80.5 %copy-start.1 = (f32[1,2048]{1,0:T(1,128)S(1)}, f32[1,2048]{1,0:T(1,128)}, u32[]{:S(2)}) copy-start(f32[1,2048]{1,0:T(1,128)} %param.6) | copy-start | bytes 24580
  69.0 80.5 %copy-start.2 = (f32[1,2048]{1,0:T(1,128)S(1)}, f32[1,2048]{1,0:T(1,128)}, u32[]{:S(2)}) copy-start(f32[1,2048]{1,0:T(1,128)} %param.7) | copy-start | bytes 24580
  69.0 81.8 %copy-start.3 = (f32[1,2048]{1,0:T(1,128)S(1)}, f32[1,2048]{1,0:T(1,128)}, u32[]{:S(2)}) copy-start(f32[1,2048]{1,0:T(1,128)} %param.5) | copy-start | bytes 24580
  150.7 39.5 %copy-start = (f32[1,2048]{1,0:T(1,128)}, f32[1,2048]{1,0:T(1,128)S(1)}, u32[]{:S(2)}) copy-start(f32[1,2048]{1,0:T(1,128)S(1)} %get-tuple-element.29) | copy-start | bytes 24580
Sparse Core Ops, SparseCore 0:
  11.1 56.2 all-reduce.4
  71.7 76.1 reduce-scatter.3
